TPU v7x, 32 devices: a whole 2x2x4 slice. The times are simulated.
32 devices in a mesh: row: 4 (over y, core), col: 8 (over z, x).
Axes of the slice: x: 2, y: 2, z: 4, core: 2. Of those that a mesh axis runs over, the one named last changes fastest.
Arguments:
- positions: float32 [512, 147], P(('row', 'col')), may hold values from -0.55 to 9.45, as said below
- coefficients: float32 [512, 147], P(('row', 'col')), may hold values from -6 to 6
- atom_pairs: int32 [2, 1176], replicated, may hold values from 0 to 48, as said below
- pair_scale: float32 [1176], replicated, may hold values from 0.5 to 2
Outputs:
- applied: float32 [512, 147], P(('row', 'col'))
Inputs may be any that keep to these rules, and one draw needn't show every extreme that they name: `atom_pairs`: every unordered pair of two different atoms stands in exactly one column, the smaller atom in row 0. `positions`: every two atoms of a geometry lie 0.6 or more apart; all geometries are displacements of one molecule.
All inputs are finite; a program needn't handle non-finite values.
Results may differ from a plain program's by a relative error of at most 0.0003.
Values sent between devices are 32-bit elements; how exact they have to be, the bound alone decides.
A program may use at most 64 MiB of HBM per device.

v0:
```python
import math

import jax
import jax.numpy as jnp
from jax import lax
from jax.sharding import PartitionSpec as P

highest = lax.Precision.HIGHEST
length_scale = 2.0
decay_rate = math.sqrt(5.0) / length_scale
outer_factor = decay_rate * decay_rate / 3.0
radial_factor = decay_rate * decay_rate


def pair_table(atom_pairs, atoms):
    atom_ids = jnp.arange(atoms, dtype=jnp.int32)[:, None]
    first = (atom_ids == atom_pairs[0][None, :]).astype(jnp.float32)
    second = (atom_ids == atom_pairs[1][None, :]).astype(jnp.float32)
    return first - second


def geometry_terms(positions, coefficients, onehot, pair_scale):
    count = positions.shape[0]
    atoms = onehot.shape[0]
    spans = jnp.dot(positions.reshape(count * 3, atoms), onehot, precision=highest).reshape(
        count, 3, -1
    )
    moves = jnp.dot(coefficients.reshape(count * 3, atoms), onehot, precision=highest).reshape(
        count, 3, -1
    )
    inverse = 1.0 / jnp.sqrt(jnp.sum(spans * spans, axis=1))
    features = pair_scale[None, :] * inverse
    weights = features * inverse * inverse
    tangents = -weights * jnp.sum(spans * moves, axis=1)
    return (features, tangents, spans, weights)


def pull_back(grads, spans, weights, onehot):
    count = grads.shape[0]
    terms = -(weights * grads)[:, None, :] * spans
    return jnp.dot(terms.reshape(count * 3, -1), onehot.T, precision=highest).reshape(count, -1)


def kernel_terms(rows_x, cols_x):
    gram = jnp.dot(rows_x, cols_x.T, precision=highest)
    sq_dist = (
        jnp.sum(rows_x * rows_x, axis=1)[:, None]
        + jnp.sum(cols_x * cols_x, axis=1)[None, :]
        - 2.0 * gram
    )
    radius = jnp.sqrt(jnp.maximum(sq_dist, 0.0))
    envelope = outer_factor * jnp.exp(-decay_rate * radius)
    return (envelope, envelope * (1.0 + decay_rate * radius))


def both_ways(rows_x, rows_u, cols_x, cols_u, tile_weight):
    envelope, direct = kernel_terms(rows_x, cols_x)
    envelope = envelope * tile_weight
    direct = direct * tile_weight
    forward = envelope * (
        jnp.dot(rows_x, cols_u.T, precision=highest) - jnp.sum(cols_x * cols_u, axis=1)[None, :]
    )
    backward = envelope * (
        jnp.dot(rows_u, cols_x.T, precision=highest) - jnp.sum(rows_x * rows_u, axis=1)[:, None]
    )
    to_rows = jnp.dot(direct, cols_u, precision=highest) - radial_factor * (
        jnp.sum(forward, axis=1)[:, None] * rows_x - jnp.dot(forward, cols_x, precision=highest)
    )
    to_cols = jnp.dot(direct.T, rows_u, precision=highest) - radial_factor * (
        jnp.sum(backward, axis=0)[:, None] * cols_x - jnp.dot(backward.T, rows_x, precision=highest)
    )
    return (to_rows, to_cols)


def kept_blocks(col_count, col_index, kept_span):
    steps = jnp.arange(kept_span, dtype=jnp.int32)
    return (col_index - steps) % col_count


def select_rows(block, col_count, col_index, kept_span):
    pieces = block.reshape(col_count, -1, block.shape[1])
    kept = jnp.take(pieces, kept_blocks(col_count, col_index, kept_span), axis=0)
    return kept.reshape(-1, block.shape[1])


def restore_rows(block, col_count, col_index, kept_span):
    pieces = block.reshape(kept_span, -1, block.shape[1])
    chosen = kept_blocks(col_count, col_index, kept_span)
    placing = (jnp.arange(col_count, dtype=jnp.int32)[:, None] == chosen[None, :]).astype(
        pieces.dtype
    )
    padded = jnp.einsum("ck,kgf->cgf", placing, pieces, precision=highest)
    return padded.reshape(-1, block.shape[1])


def fold_weights(row_count, col_count, row_index, col_index, per_device):
    kept_half = col_count // 2
    offsets = jnp.arange(kept_half + 1, dtype=jnp.int32)[:, None]
    partner = jnp.arange(row_count, dtype=jnp.int32)[None, :]
    apart = (partner - row_index) % row_count
    first = jnp.where(
        apart == 0,
        0.5,
        jnp.where(
            (apart >= 1) & (apart < row_count // 2),
            1.0,
            jnp.where((apart == row_count // 2) & (row_index < partner), 1.0, 0.0),
        ),
    )
    middle = jnp.where(
        (row_index < partner) | (row_index == partner) & (col_index < kept_half), 1.0, 0.0
    )
    chosen = jnp.where(offsets == 0, first, jnp.where(offsets == kept_half, middle, 1.0)).astype(
        jnp.float32
    )
    spread = jnp.broadcast_to(
        chosen[:, None, :, None], (kept_half + 1, per_device, row_count, per_device)
    )
    return spread.reshape((kept_half + 1) * per_device, row_count * per_device)


def on_device(positions, coefficients, atom_pairs, pair_scale):
    row_count = lax.axis_size("row")
    col_count = lax.axis_size("col")
    row_index = lax.axis_index("row")
    col_index = lax.axis_index("col")
    per_device = positions.shape[0]
    atoms = positions.shape[1] // 3
    kept_span = col_count // 2 + 1
    onehot = pair_table(atom_pairs, atoms)
    tile_weight = fold_weights(row_count, col_count, row_index, col_index, per_device)
    features, tangents, spans, weights = geometry_terms(positions, coefficients, onehot, pair_scale)
    rows_x, rows_u = (
        lax.all_gather(features, "col", axis=0, tiled=True),
        lax.all_gather(tangents, "col", axis=0, tiled=True),
    )
    cols_x, cols_u = (
        lax.all_gather(features, "row", axis=0, tiled=True),
        lax.all_gather(tangents, "row", axis=0, tiled=True),
    )
    rows_x = select_rows(rows_x, col_count, col_index, kept_span)
    rows_u = select_rows(rows_u, col_count, col_index, kept_span)
    to_rows, to_cols = both_ways(rows_x, rows_u, cols_x, cols_u, tile_weight)
    own_rows = lax.psum_scatter(
        restore_rows(to_rows, col_count, col_index, kept_span),
        "col",
        scatter_dimension=0,
        tiled=True,
    )
    own_cols = lax.psum_scatter(to_cols, "row", scatter_dimension=0, tiled=True)
    return pull_back(own_rows + own_cols, spans, weights, onehot)


def solution(mesh):
    in_specs = (P(("row", "col"), None), P(("row", "col"), None), P(), P())
    out_specs = P(("row", "col"), None)
    return jax.shard_map(
        on_device, mesh=mesh, in_specs=in_specs, out_specs=out_specs, check_vma=False
    )
```

profile of v0, /device:TPU:0, one launch (start us, length us, event | category | flops | bytes accessed | tf_op | source)
XLA Modules:
  0.0 188.8 jit_solution(1568657946876916223)
XLA Ops:
  6.6 0.8 slice_reduce_fusion.1
  7.5 0.6 copy-done.2
  8.2 0.4 fusion.32
  8.6 0.4 fusion.2
  9.1 0.1 mul.143
  9.3 0.2 reduce_sum.75
  9.5 0.2 reduce_sum.72
  9.7 0.5 copy-done
  10.2 33.5 %all_gather.12 = f32[128,1176]{1,0:T(8,128)S(1)} all-gather(f32[16,1176]{1,0:T(8,128)S(1)} %get-tuple-element.14), channel_id=1, replica_groups=mesh['row'=4,'col'=8] {'col'}, dimensions={0}, use_global_device_ids=true | all-gather | bytes 677376 | tf_op jit(solution)/shard_map/all_gather | solution.py:134
  43.7 6.0 %all_gather.13 = f32[64,1176]{1,0:T(8,128)S(1)} all-gather(f32[16,1176]{1,0:T(8,128)S(1)} %get-tuple-element.14), channel_id=1, replica_groups=mesh['row'=4,'col'=8] {'row'}, dimensions={0}, use_global_device_ids=true | all-gather | bytes 376320 | tf_op jit(solution)/shard_map/all_gather | solution.py:138
  49.7 31.7 %all_gather.15 = f32[128,1176]{1,0:T(8,128)S(1)} all-gather(f32[16,1176]{1,0:T(8,128)S(1)} %get-tuple-element.15), channel_id=1, replica_groups=mesh['row'=4,'col'=8] {'col'}, dimensions={0}, use_global_device_ids=true | all-gather | bytes 677376 | tf_op jit(solution)/shard_map/all_gather | solution.py:135
  81.5 5.9 %all_gather.14 = f32[64,1176]{1,0:T(8,128)S(1)} all-gather(f32[16,1176]{1,0:T(8,128)S(1)} %get-tuple-element.15), channel_id=1, replica_groups=mesh['row'=4,'col'=8] {'row'}, dimensions={0}, use_global_device_ids=true | all-gather | bytes 376320 | tf_op jit(solution)/shard_map/all_gather | solution.py:139
  87.4 0.6 gather_fusion
  88.0 0.6 gather_fusion.1
  88.6 0.2 multiply_reduce_fusion
  89.2 0.1 reshape.189
  89.4 0.2 multiply_reduce_fusion.3
  89.5 0.5 fusion.7
  90.1 0.6 fusion.34
  90.6 0.4 fusion.1
  91.1 1.2 convolution_subtract_fusion.3
  92.3 0.5 fusion.33
  92.8 0.5 fusion
  93.4 0.5 convolution_subtract_fusion.1
  93.9 0.7 fusion.8
  94.6 1.0 copy.9
  95.7 18.0 %reduce-scatter.5.cloned.1.call-done = f32[16,1176]{1,0:T(8,128)} async-done(((f32[64,1176]{1,0:T(8,128)}), f32[16,1176]{1,0:T(8,128)}) %reduce-scatter.5.cloned.1.call-update) | async-done | bytes 75280 | tf_op jit(solution)/shard_map/reduce_scatter | solution.py:150
  113.6 66.1 %reduce-scatter.3.cloned.1.call-done = f32[16,1176]{1,0:T(8,128)} async-done(((f32[128,1176]{1,0:T(8,128)}), f32[16,1176]{1,0:T(8,128)}) %reduce-scatter.3.cloned.1.call-update) | async-done | bytes 75280 | tf_op jit(solution)/shard_map/reduce_scatter | solution.py:144
  179.7 1.0 multiply_negate_fusion
  180.7 0.1 mul.160
  180.9 0.4 fusion.10
  181.3 0.7 reshape.195
  (24 shorter events, 0.9 us)
Async XLA Ops:
  6.5 107.1 %reduce-scatter.5.cloned.1.call-start = ((), (), s32[]{:S(2)}) async-start(), calls=%async_computation.3 | async-start | bytes 409600 | tf_op jit(solution)/shard_map/reduce_scatter | solution.py:150
  6.5 0.8 copy-start.1
  7.4 0.7 copy-start.2
  9.5 0.7 copy-start
  92.3 87.4 %reduce-scatter.3.cloned.1.call-start = ((), (), s32[]{:S(2)}) async-start(), calls=%async_computation.2 | async-start | bytes 737280 | tf_op jit(solution)/shard_map/reduce_scatter | solution.py:144
Sparse Core Ops, SparseCore 0:
  92.4 21.1 reduce-scatter.4
  116.9 62.7 reduce-scatter.2
where the time goes:
time: 189 us
  waiting for transfers between devices  84.1 us (44%)
  blocking collectives  77.2 us (41%)
  between operations  13.6 us (7%)
  matrix products  6.19 us (3%)
  local copies, waits for them, and re-layouts  5.79 us (3%)
    reduce_scatter x1, waiting for transfers between devices, on_device(): lax.psum_scatter(restore_rows(to_rows, col_count, col_index, kept_span),...  66.1 us
    all_gather x1, blocking collectives, on_device(): lax.all_gather(features, 'col', axis=0, tiled=True)  33.5 us
    all_gather x1, blocking collectives, on_device(): lax.all_gather(tangents, 'col', axis=0, tiled=True)  31.7 us
    reduce_scatter x1, waiting for transfers between devices, on_device(): own_cols = lax.psum_scatter(to_cols, 'row', scatter_dimension=0, tiled=True)  18 us
    all_gather x1, blocking collectives, on_device(): lax.all_gather(features, 'row', axis=0, tiled=True)  6.05 us
    all_gather x1, blocking collectives, on_device(): lax.all_gather(tangents, 'row', axis=0, tiled=True)  5.94 us
  transfers between devices with their start and end apart: 2, of which 2 were waited for; matrix products, arithmetic and copies ran while one was open for 2% of the time, Pallas kernels for 0%

commit v1 on v0

v1 whole, which is shorter than its diff:
```python
import functools
import math

import jax
import jax.numpy as jnp
from jax import lax
from jax.experimental import pallas as pl
from jax.experimental.pallas import tpu as pltpu
from jax.sharding import PartitionSpec as P

length_scale = 2.0
decay_rate = math.sqrt(5.0) / length_scale
outer_factor = decay_rate * decay_rate / 3.0
radial_factor = decay_rate * decay_rate

LANES = 128
HALF = 64
TILE = 256
f32, bf16 = jnp.float32, jnp.bfloat16


def dot(a, b):
    return jnp.dot(a, b, preferred_element_type=f32)


def rounded(v):
    return v.astype(bf16).astype(f32)


def two_parts(v):
    hi = v.astype(bf16)
    return hi, (v - hi.astype(f32)).astype(bf16)


def operands(packed):
    hi = rounded(packed)
    rest = packed - hi
    mid = rounded(rest)
    low = pltpu.roll(rest - mid, HALF, 1)
    first = lax.broadcasted_iota(jnp.int32, packed.shape, 1) < HALF
    hi = hi.astype(bf16)
    for_spans = jnp.concatenate([hi, jnp.where(first, mid, low).astype(bf16)], axis=1)
    for_moves = jnp.concatenate([hi, jnp.where(first, low, mid).astype(bf16)], axis=1)
    return for_spans, for_moves


def kernel(
    row_count, col_count, per, atoms, width,
    pos_ref, coef_ref, pairs_ref, scale_ref, out_ref,
    gathered, pairs, scale, table_s, table_m, own_s, own_x, own_w, own_t, hold_x, hold_u, acc, bent_sum,
    send_col, recv_col, send_row, recv_row,
):
    row = lax.axis_index("row")
    col = lax.axis_index("col")
    padded = table_s.shape[1]
    block = 3 * per
    count = col_count * per
    halves = row_count // 2 if row_count % 2 == 0 else row_count
    cores = row_count // halves

    def row_peer(k, sign):
        ky, kc = k // cores, k % cores
        y, c = row // cores, row % cores
        if sign > 0:
            return lax.rem(y + ky, halves) * cores + lax.rem(c + kc, cores)
        return lax.rem(y + halves - ky, halves) * cores + lax.rem(c + cores - kc, cores)

    barrier = pltpu.get_barrier_semaphore()
    for s in range(1, col_count):
        pl.semaphore_signal(
            barrier, inc=1, device_id=(row, lax.rem(col + s, col_count)), device_id_type=pl.DeviceIdType.MESH
        )
    for k in range(1, row_count):
        pl.semaphore_signal(
            barrier, inc=1, device_id=(row_peer(k, 1), col), device_id_type=pl.DeviceIdType.MESH
        )

    position, coefficient = pos_ref[...], coef_ref[...]
    gap = jnp.zeros((per, HALF - atoms), f32)
    for k in range(3):
        cut = slice(k * atoms, (k + 1) * atoms)
        gathered[0, k * per : (k + 1) * per, :] = jnp.concatenate(
            [position[:, cut], gap, coefficient[:, cut], gap], axis=1
        )
    pl.semaphore_wait(barrier, col_count - 1 + row_count - 1)

    spread = []
    for s in range(1, col_count):
        spread.append(
            pltpu.make_async_remote_copy(
                src_ref=gathered.at[0, pl.ds(0, block)],
                dst_ref=gathered.at[0, pl.ds(s * block, block)],
                send_sem=send_col.at[s],
                recv_sem=recv_col.at[s],
                device_id=(row, lax.rem(col + col_count - s, col_count)),
                device_id_type=pl.DeviceIdType.MESH,
            )
        )
    for copy in spread:
        copy.start()

    pairs[...] = jnp.full(pairs.shape, -1, jnp.int32)
    pairs[0:2, 0:width] = pairs_ref[...]
    scale[...] = jnp.zeros(scale.shape, f32)
    scale[0:1, 0:width] = scale_ref[...]
    ids = lax.broadcasted_iota(jnp.int32, (HALF, padded), 0)
    signs = (jnp.where(ids == pairs[0:1, :], 1.0, 0.0) - jnp.where(ids == pairs[1:2, :], 1.0, 0.0)).astype(bf16)
    blank = jnp.zeros((HALF, padded), bf16)
    for q in range(4):
        table_s[q * HALF : (q + 1) * HALF, :] = blank if q == 1 else signs
        table_m[q * HALF : (q + 1) * HALF, :] = blank if q == 0 else signs

    def terms(for_spans, for_moves, geoms, t):
        cut = slice(t * TILE, (t + 1) * TILE)
        spans = dot(for_spans, table_s[:, cut]).reshape(geoms, 3, per, TILE)
        moves = dot(for_moves, table_m[:, cut]).reshape(geoms, 3, per, TILE)
        square = spans[:, 0] * spans[:, 0] + spans[:, 1] * spans[:, 1] + spans[:, 2] * spans[:, 2]
        inner = spans[:, 0] * moves[:, 0] + spans[:, 1] * moves[:, 1] + spans[:, 2] * moves[:, 2]
        square = square.reshape(geoms * per, TILE)
        inner = inner.reshape(geoms * per, TILE)
        if (t + 1) * TILE > width:
            lane = lax.broadcasted_iota(jnp.int32, square.shape, 1)
            square = jnp.where(lane < width - t * TILE, square, 1.0)
        inverse = lax.rsqrt(square)
        features = scale[0:1, cut] * inverse
        weights = features * inverse * inverse
        return spans, features, weights, -weights * inner

    for_spans, for_moves = operands(gathered[0, 0:block, :])
    own_square = jnp.zeros((per, 1), f32)
    for t in range(padded // TILE):
        cut = slice(t * TILE, (t + 1) * TILE)
        spans, features, weights, _ = terms(for_spans, for_moves, 1, t)
        own_s[:, cut] = spans.reshape(block, TILE)
        own_x[:, cut] = features
        own_w[:, cut] = weights
        own_square += jnp.sum(features * features, axis=1, keepdims=True)
        hi = rounded(features)
        stacked = jnp.concatenate([hi, features - hi, jnp.zeros((LANES - 2 * per, TILE), f32)], axis=0)
        own_t[cut, :] = stacked.T.astype(bf16)
    acc[...] = jnp.zeros(acc.shape, f32)
    bent_sum[...] = jnp.zeros(bent_sum.shape, f32)

    for copy in spread:
        copy.wait_recv()
    pushed = []
    for k in range(1, row_count):
        pushed.append(
            pltpu.make_async_remote_copy(
                src_ref=gathered.at[0],
                dst_ref=gathered.at[k],
                send_sem=send_row.at[k],
                recv_sem=recv_row.at[k],
                device_id=(row_peer(k, -1), col),
                device_id_type=pl.DeviceIdType.MESH,
            )
        )
    for copy in pushed:
        copy.start()

    def one_chunk(k, carry):
        @pl.when(k > 0)
        def _():
            pltpu.make_async_remote_copy(
                src_ref=gathered.at[0],
                dst_ref=gathered.at[k],
                send_sem=send_row.at[k],
                recv_sem=recv_row.at[k],
                device_id=(row, col),
                device_id_type=pl.DeviceIdType.MESH,
            ).wait_recv()

        for_spans, for_moves = operands(gathered[k])
        square = jnp.zeros((count, LANES), f32)
        mixed = jnp.zeros((count, LANES), f32)
        for t in range(padded // TILE):
            cut = slice(t * TILE, (t + 1) * TILE)
            _, features, _, tangents = terms(for_spans, for_moves, col_count, t)
            for part in range(TILE // LANES):
                x = features[:, part * LANES : (part + 1) * LANES]
                u = tangents[:, part * LANES : (part + 1) * LANES]
                square += x * x
                mixed += x * u
            hi, low = two_parts(features)
            hold_x[0:count, cut] = hi
            hold_x[count : 2 * count, cut] = low
            hi, low = two_parts(tangents)
            hold_u[0:count, cut] = hi
            hold_u[count : 2 * count, cut] = low
        turned = own_t[...]
        gram = dot(hold_x[...], turned)
        gram = (gram[0:count] + gram[count : 2 * count]).T
        gram = gram[0:per] + gram[per : 2 * per]
        cross = dot(hold_u[...], turned)
        cross = (cross[0:count] + cross[count : 2 * count]).T
        cross = cross[0:per] + cross[per : 2 * per]
        square = jnp.sum(square.T, axis=0, keepdims=True)
        mixed = jnp.sum(mixed.T, axis=0, keepdims=True)
        radius = jnp.sqrt(jnp.maximum(own_square + square - 2.0 * gram, 0.0))
        envelope = outer_factor * jnp.exp(-decay_rate * radius)
        direct = envelope * (1.0 + decay_rate * radius)
        bent = radial_factor * (envelope * (cross - mixed))
        bent_sum[...] += jnp.broadcast_to(jnp.sum(bent, axis=1, keepdims=True), bent_sum.shape)

        def doubled(v):
            hi = rounded(v)
            both = jnp.concatenate([hi, v - hi], axis=0).astype(bf16)
            return jnp.concatenate([both, both], axis=1)

        acc[...] += dot(doubled(direct), hold_u[...]) + dot(doubled(bent), hold_x[...])
        return carry

    lax.fori_loop(0, row_count, one_chunk, 0)

    grads = acc[0:per, :] + acc[per : 2 * per, :] - bent_sum[:, 0:1] * own_x[...]
    pulled = -(own_w[...] * grads)
    pieces = []
    for k in range(3):
        pieces.append(pulled * own_s[k * per : (k + 1) * per, :])
    whole = jnp.concatenate(pieces, axis=0)
    hi = rounded(whole)
    mid = rounded(whole - hi)
    stacked = jnp.concatenate([hi, mid, whole - hi - mid], axis=0).astype(bf16)
    result = lax.dot_general(
        stacked, table_s[0:LANES, :], (((1,), (1,)), ((), ())), preferred_element_type=f32
    )
    result = result[0:block] + result[block : 2 * block] + result[2 * block : 3 * block]
    out_ref[...] = jnp.concatenate([result[k * per : (k + 1) * per, 0:atoms] for k in range(3)], axis=1)
    for copy in spread + pushed:
        copy.wait_send()


def on_device(positions, coefficients, atom_pairs, pair_scale):
    row_count = lax.axis_size("row")
    col_count = lax.axis_size("col")
    per = positions.shape[0]
    atoms = positions.shape[1] // 3
    width = atom_pairs.shape[1]
    padded = -(-width // TILE) * TILE
    count = col_count * per
    vmem = pl.BlockSpec(memory_space=pltpu.VMEM)
    return pl.pallas_call(
        functools.partial(kernel, row_count, col_count, per, atoms, width),
        out_shape=jax.ShapeDtypeStruct(positions.shape, f32),
        in_specs=[vmem] * 4,
        out_specs=vmem,
        scratch_shapes=[
            pltpu.VMEM((row_count, col_count * 3 * per, LANES), f32),
            pltpu.VMEM((8, padded), jnp.int32),
            pltpu.VMEM((8, padded), f32),
            pltpu.VMEM((TILE, padded), bf16),
            pltpu.VMEM((TILE, padded), bf16),
            pltpu.VMEM((3 * per, padded), f32),
            pltpu.VMEM((per, padded), f32),
            pltpu.VMEM((per, padded), f32),
            pltpu.VMEM((padded, LANES), bf16),
            pltpu.VMEM((2 * count, padded), bf16),
            pltpu.VMEM((2 * count, padded), bf16),
            pltpu.VMEM((2 * per, padded), f32),
            pltpu.VMEM((per, LANES), f32),
            pltpu.SemaphoreType.DMA((col_count,)),
            pltpu.SemaphoreType.DMA((col_count,)),
            pltpu.SemaphoreType.DMA((row_count,)),
            pltpu.SemaphoreType.DMA((row_count,)),
        ],
        compiler_params=pltpu.CompilerParams(
            collective_id=0, has_side_effects=True, vmem_limit_bytes=48 * 1024 * 1024
        ),
    )(positions, coefficients, atom_pairs, pair_scale.reshape(1, width))


def solution(mesh):
    in_specs = (P(("row", "col"), None), P(("row", "col"), None), P(), P())
    out_specs = P(("row", "col"), None)
    return jax.shard_map(
        on_device, mesh=mesh, in_specs=in_specs, out_specs=out_specs, check_vma=False
    )
```

time: 189 us -> 26.1 us (0.14)
  the two profiles are of different devices: /device:TPU:0 before, /device:TPU:1 now
where the time goes in v1:
time: 26.1 us; the launch traced here: 25.6 us
  Pallas kernels  22.9 us (88%)
  local copies, waits for them, and re-layouts  2.76 us (11%)
    pallas_call x1, Pallas kernels, on_device(): pl.pallas_call(functools.partial(kernel, row_count, col_count, per, atoms...  22.9 us
    unnamed x7, local copies, waits for them, and re-layouts  2.04 us
    reshape x1, local copies, waits for them, and re-layouts, on_device(): pair_scale.reshape(1, width)  0.71 us

profile of v1, /device:TPU:1, one launch (start us, length us, event | category | flops | bytes accessed | tf_op | source)
XLA Modules:
  0.0 25.6 jit_solution(18773255248329065)
XLA Ops:
  0.0 0.0 copy-start.2
  0.0 0.7 %reshape.3.scale_ref = f32[1,1176]{1,0:T(1,128)S(1)} reshape(f32[1176]{0:T(1024)} %param.7) | data formatting | bytes 9408 | tf_op jit(solution)/shard_map/reshape | solution.py:269
  0.7 0.0 copy-done.2
  0.7 0.0 copy-start
  0.7 0.7 %copy-done = f32[16,147]{1,0:T(8,128)S(1)} copy-done((f32[16,147]{1,0:T(8,128)S(1)}, f32[16,147]{1,0:T(8,128)}, u32[]{:S(2)}) %copy-start) | copy-done | bytes 9432
  1.4 0.0 copy-start.1
  1.4 0.7 %copy-done.1 = f32[16,147]{1,0:T(8,128)S(1)} copy-done((f32[16,147]{1,0:T(8,128)S(1)}, f32[16,147]{1,0:T(8,128)}, u32[]{:S(2)}) %copy-start.1) | copy-done | bytes 9432
  2.2 22.9 %shard_map.46 = f32[16,147]{1,0:T(8,128)S(1)} custom-call(f32[16,147]{1,0:T(8,128)S(1)} %copy-done, f32[16,147]{1,0:T(8,128)S(1)} %copy-done.1, s32[2,1176]{1,0:T(2,128)S(1)} %copy-done.2, f32[1,1176]{1,0:T(1,128)S(1)} %reshape.3.scale_ref), custom_call_target="tpu_custom_call" | custom-call | tf_op jit(solution)/shard_map/pallas_call | solution.py:242
  25.0 0.6 %copy.6 = f32[16,147]{1,0:T(8,128)} copy(f32[16,147]{1,0:T(8,128)S(1)} %shard_map.46) | data formatting | bytes 18816
Async XLA Ops:
  0.0 0.7 %copy-start.2 = (s32[2,1176]{1,0:T(2,128)S(1)}, s32[2,1176]{1,0:T(2,128)}, u32[]{:S(2)}) copy-start(s32[2,1176]{1,0:T(2,128)} %pairs_ref.1) | copy-start | bytes 28228
  0.7 0.7 %copy-start = (f32[16,147]{1,0:T(8,128)S(1)}, f32[16,147]{1,0:T(8,128)}, u32[]{:S(2)}) copy-start(f32[16,147]{1,0:T(8,128)} %pos_ref.1) | copy-start | bytes 28228
  1.4 0.7 %copy-start.1 = (f32[16,147]{1,0:T(8,128)S(1)}, f32[16,147]{1,0:T(8,128)}, u32[]{:S(2)}) copy-start(f32[16,147]{1,0:T(8,128)} %coef_ref.1) | copy-start | bytes 28228
